TPU v7x, 256 devices: a whole 4x4x8 slice. The times are simulated.
256 devices in a mesh: seq: 32 (over z_hi, x, core), ch: 8 (over z_lo, y).
Axes of the slice: x: 4, y: 4, z: 8 (z_hi: 4, z_lo: 2; z = z_hi * 2 + z_lo), core: 2. Of those that a mesh axis runs over, the one named last changes fastest.
Arguments:
- query_act: bfloat16 [4096, 4096], P('seq', 'ch'), may hold values from -6 to 6
- key_act: bfloat16 [4096, 4096], P('seq', 'ch'), may hold values from -6 to 6
- value_act: bfloat16 [4096, 4096], P('seq', 'ch'), may hold values from -6 to 6
- filter_taps: bfloat16 [4096, 4096], P('seq', 'ch'), may hold values from -2 to 2
- out_grad: bfloat16 [4096, 4096], P('seq', 'ch'), may hold values from -6 to 6
- out_weight: bfloat16 [4096, 4096], P('ch'), may hold values from -0.09375 to 0.09375
Outputs:
- mixed_out: bfloat16 [4096, 4096], P('seq', 'ch')
- query_grad: bfloat16 [4096, 4096], P('seq', 'ch')
- key_grad: bfloat16 [4096, 4096], P('seq', 'ch')
- value_grad: bfloat16 [4096, 4096], P('seq', 'ch')
- filter_grad: float32 [4096, 4096], P('seq', 'ch')
All inputs are finite; a program needn't handle non-finite values.
Results may differ from a plain program's by a relative error of at most 0.02.
Values may be sent and summed in bfloat16 or wider, within the bound.
A program may use at most 128 MiB of HBM per device.

v0:
```python
import math
import jax
import jax.numpy as jnp
from jax import lax
from jax.sharding import PartitionSpec as P


def dft_tables(span_rows):
    period = 2 * span_rows
    frequency = jnp.arange(span_rows, dtype=jnp.int32)
    times_in = jnp.arange(span_rows, dtype=jnp.int32)
    times_out = jnp.arange(period, dtype=jnp.int32)
    parity_in = 1.0 - 2.0 * (times_in % 2).astype(jnp.float32)
    parity_out = 1.0 - 2.0 * (times_out % 2).astype(jnp.float32)
    phase_in = (frequency[:, None] * times_in[None, :] % period).astype(jnp.float32) * (
        2.0 * math.pi / period
    )
    cosine_rows = jnp.cos(phase_in)
    sine_rows = jnp.where(frequency[:, None] == 0, parity_in[None, :], -jnp.sin(phase_in))
    forward_t = jnp.concatenate([cosine_rows, sine_rows], axis=0)
    phase_out = (times_out[:, None] * frequency[None, :] % period).astype(jnp.float32) * (
        2.0 * math.pi / period
    )
    scaling = jnp.where(frequency == 0, 1.0, 2.0).astype(jnp.float32) / period
    cosinus_table_entries = jnp.cos(phase_out) * scaling[None, :]
    sine_cols = jnp.where(
        frequency[None, :] == 0,
        parity_out[:, None] / period,
        -jnp.sin(phase_out) * scaling[None, :],
    )
    inverse_t = jnp.concatenate([cosinus_table_entries, sine_cols], axis=1)
    alternate = 1.0 - 2.0 * (frequency % 2).astype(jnp.float32)
    top_sign = 1.0 - 2.0 * float(span_rows % 2)
    shift_sign = jnp.concatenate([alternate, jnp.where(frequency == 0, top_sign, alternate)])[
        :, None
    ]
    pair_mask = (frequency > 0).astype(jnp.float32)[:, None]
    return (forward_t, inverse_t, shift_sign, pair_mask)


def split_table(forward_t):
    table_high = forward_t.astype(jnp.bfloat16)
    kept_high = lax.optimization_barrier(table_high)
    table_low = (forward_t - kept_high.astype(jnp.float32)).astype(jnp.bfloat16)
    return (table_high, table_low)


def packed_product(first_spec, second_spec, pair_mask, conjugate):
    half_rows = first_spec.shape[-2] // 2
    first_real = first_spec[..., :half_rows, :]
    leading_quadrature_term = first_spec[..., half_rows:, :]
    second_real = second_spec[..., :half_rows, :]
    second_imag = second_spec[..., half_rows:, :]
    cross_real = leading_quadrature_term * second_imag
    if conjugate:
        real_part = first_real * second_real + pair_mask * cross_real
        imag_part = (
            pair_mask * (first_real * second_imag - leading_quadrature_term * second_real)
            + (1.0 - pair_mask) * cross_real
        )
    else:
        real_part = first_real * second_real - pair_mask * cross_real
        imag_part = (
            pair_mask * (first_real * second_imag + leading_quadrature_term * second_real)
            + (1.0 - pair_mask) * cross_real
        )
    return jnp.concatenate([real_part, imag_part], axis=-2)


def grouped_sums(spec_u, spec_h, spec_g, own_index, shift_sign, pair_mask):
    block_count = spec_u.shape[0]
    group_width = 8
    zero_spec = jnp.zeros(spec_u.shape[1:], jnp.float32)

    def fetch(spec, indices, usable):
        picked = spec[jnp.clip(indices, 0, block_count - 1)].astype(jnp.float32)
        return jnp.where(usable[:, None, None], picked, 0.0)

    def group_step(group, carry):
        conv_acc, ugrad_acc, hgrad_acc = carry
        indices = group * group_width + jnp.arange(group_width, dtype=jnp.int32)
        u_now = spec_u[indices].astype(jnp.float32)
        h_now = spec_h[indices].astype(jnp.float32)
        u_prev = fetch(spec_u, indices - 1, indices >= 1)
        lag = own_index - indices
        h_lag = fetch(spec_h, lag, lag >= 0)
        conv_acc = conv_acc + jnp.sum(
            packed_product(u_prev + shift_sign * u_now, h_lag, pair_mask, False), axis=0
        )
        lead = own_index + indices
        g_lead = fetch(spec_g, lead, lead <= block_count - 1)
        g_next = fetch(spec_g, lead + 1, lead + 1 <= block_count - 1)
        ahead = g_lead + shift_sign * g_next
        ugrad_acc = ugrad_acc + jnp.sum(packed_product(h_now, ahead, pair_mask, True), axis=0)
        hgrad_acc = hgrad_acc + jnp.sum(packed_product(u_now, ahead, pair_mask, True), axis=0)
        return (conv_acc, ugrad_acc, hgrad_acc)

    return lax.fori_loop(
        0, block_count // group_width, group_step, (zero_spec, zero_spec, zero_spec)
    )


def transform(blocks, table_high, table_low):
    high_part = jnp.einsum("pt,ntc->npc", table_high, blocks, preferred_element_type=jnp.float32)
    low_part = jnp.einsum("pt,ntc->npc", table_low, blocks, preferred_element_type=jnp.float32)
    return (high_part + low_part).astype(jnp.bfloat16)


def own_block(spec_u, spec_h, spec_g, own_index, inverse_t, shift_sign, pair_mask, span_rows):
    conv_spec, ugrad_spec, hgrad_spec = grouped_sums(
        spec_u, spec_h, spec_g, own_index, shift_sign, pair_mask
    )
    conv = jnp.dot(inverse_t[span_rows:], conv_spec, precision=lax.Precision.HIGHEST)
    u_grad = jnp.dot(inverse_t[:span_rows], ugrad_spec, precision=lax.Precision.HIGHEST)
    filter_grad = jnp.dot(inverse_t[:span_rows], hgrad_spec, precision=lax.Precision.HIGHEST)
    return (conv, u_grad, filter_grad)


def per_device(query_act, key_act, value_act, filter_taps, out_grad, out_weight):
    span_rows, feature_count = query_act.shape
    block_count = lax.axis_size("seq")
    own_index = lax.axis_index("seq")
    forward_t, inverse_t, shift_sign, pair_mask = dft_tables(span_rows)
    table_high, table_low = split_table(forward_t)
    product = (key_act.astype(jnp.float32) * value_act.astype(jnp.float32)).astype(jnp.bfloat16)
    gated_grad = lax.dot_general(
        lax.all_gather(out_grad, "ch", axis=1, tiled=True),
        out_weight,
        (((1,), (1,)), ((), ())),
        preferred_element_type=jnp.float32,
    )
    conv_grad = (gated_grad * query_act.astype(jnp.float32)).astype(jnp.bfloat16)
    own_u = transform(product[None], table_high, table_low)[0]
    own_h = transform(filter_taps[None], table_high, table_low)[0]
    own_g = transform(conv_grad[None], table_high, table_low)[0]
    received = (
        lax.all_gather(own_u, "seq", axis=0, tiled=True),
        lax.all_gather(own_h, "seq", axis=0, tiled=True),
        lax.all_gather(own_g, "seq", axis=0, tiled=True),
    )
    spec_u, spec_h, spec_g = [
        series.reshape(block_count, 2 * span_rows, feature_count) for series in received
    ]
    conv, u_grad, filter_grad = own_block(
        spec_u, spec_h, spec_g, own_index, inverse_t, shift_sign, pair_mask, span_rows
    )
    gated = (query_act.astype(jnp.float32) * conv).astype(jnp.bfloat16)
    partial_out = jnp.dot(gated, out_weight, preferred_element_type=jnp.float32)
    mixed_out = lax.psum_scatter(
        partial_out.astype(jnp.bfloat16), "ch", scatter_dimension=1, tiled=True
    )
    query_grad = (gated_grad * conv).astype(jnp.bfloat16)
    key_grad = (u_grad * value_act.astype(jnp.float32)).astype(jnp.bfloat16)
    value_grad = (u_grad * key_act.astype(jnp.float32)).astype(jnp.bfloat16)
    return (mixed_out, query_grad, key_grad, value_grad, filter_grad)


def solution(mesh):
    return jax.shard_map(
        per_device,
        mesh=mesh,
        in_specs=(
            P("seq", "ch"),
            P("seq", "ch"),
            P("seq", "ch"),
            P("seq", "ch"),
            P("seq", "ch"),
            P("ch", None),
        ),
        out_specs=(P("seq", "ch"), P("seq", "ch"), P("seq", "ch"), P("seq", "ch"), P("seq", "ch")),
        check_vma=False,
    )
```

profile of v0, /device:TPU:2, one launch (start us, length us, event | category | flops | bytes accessed | tf_op | source)
XLA Modules:
  0.0 563.4 jit_solution(4437507908320917075)
XLA Ops:
  8.3 1.2 fusion.43
  9.5 1.9 fusion.19
  11.6 42.8 %all-gather.9.cloned.1.call-done = bf16[128,4096]{1,0:T(8,128)(2,1)} async-done(((bf16[128,512]{1,0:T(8,128)(2,1)}), bf16[128,4096]{1,0:T(8,128)(2,1)}) %all-gather.9.cloned.1.call-update) | async-done | bytes 1048592 | tf_op jit(solution)/shard_map/all_gather | solution.py:127
  54.4 4.0 fusion.62
  61.7 1.2 multiply_select_fusion
  62.9 78.3 %all-gather.11.cloned.1.call-done = bf16[1,8192,512]{1,2,0:T(8,128)(2,1)} async-done(((bf16[1,256,512]{1,2,0:T(8,128)(2,1)}), bf16[1,8192,512]{1,2,0:T(8,128)(2,1)}) %all-gather.11.cloned.1.call-update) | async-done | bytes 8388624 | tf_op jit(solution)/shard_map/all_gather | solution.py:137
  141.2 11.6 %copy.13 = bf16[1,8192,512]{2,1,0:T(8,128)(2,1)} copy(bf16[1,8192,512]{1,2,0:T(8,128)(2,1)} %all-gather.11.cloned.1.call-done) | data formatting | bytes 16777216
  152.9 74.7 %all-gather.13.cloned.1.call-done = bf16[1,8192,512]{1,2,0:T(8,128)(2,1)} async-done(((bf16[1,256,512]{1,2,0:T(8,128)(2,1)}), bf16[1,8192,512]{1,2,0:T(8,128)(2,1)}) %all-gather.13.cloned.1.call-update) | async-done | bytes 8388624 | tf_op jit(solution)/shard_map/all_gather | solution.py:139
  227.5 12.0 %copy.14 = bf16[1,8192,512]{2,1,0:T(8,128)(2,1)} copy(bf16[1,8192,512]{1,2,0:T(8,128)(2,1)} %all-gather.13.cloned.1.call-done) | data formatting | bytes 16777216
  239.6 67.1 %all-gather.7.cloned.1.call-done = bf16[8192,512]{1,0:T(8,128)(2,1)} async-done(((bf16[256,512]{1,0:T(8,128)(2,1)}), bf16[8192,512]{1,0:T(8,128)(2,1)}) %all-gather.7.cloned.1.call-update) | async-done | bytes 8388624 | tf_op jit(solution)/shard_map/all_gather | solution.py:138
  306.7 203.5 %while.21 = (s32[]{:T(128)}, f32[256,512]{1,0:T(8,128)S(1)}, f32[256,512]{1,0:T(8,128)}, f32[256,512]{1,0:T(8,128)}, bf16[32,256,512]{2,1,0:T(8,128)(2,1)}, /*in...) while((s32[]{:T(128)}, f32[256,512]{1,0:T(8,128)S(1)}, ...), condition=%wide.region_4.5_spmd.clone.clone, body=%wide.region_0.4_spmd.clone.clone.sunk | while | flops 38148044 | bytes 155214800 | solution.py:98
  306.7 4.1 gather_fusion
  310.8 2.7 convert_select_fusion.2
  313.6 5.3 gather_fusion.1
  318.9 5.4 gather_fusion.2
  324.4 4.1 gather_fusion.3
  328.5 5.4 gather_fusion.4
  333.9 6.7 %multiply_add_fusion.9 = (f32[8,256,512]{2,1,0:T(8,128)}, f32[8,256,512]{2,1,0:T(8,128)S(1)}) fusion(bf16[8,256,512]{2,1,0:T(8,128)(2,1)} %gather_fusion.1, bf16[8,256,512]{2,1,0:T(8,128)(2,1)} %gather_fusion.2, f32[256]{0:T(256)S(1)} %get-tuple-element.514, pred[8]{0:T(512)(128)(4,1)S(1)} %add_compare_fusion.2, pred[8]{0:T(512)(128)(4,1)S(1)} %fusion.88, ...), kind=kLoop, calls=%fused_computation.11.clone.1 | loop fusion | flops 11534336 | bytes 16778264 | tf_op jit(solution)/shard_map/while/body/eval_jaxpr/add | solution.py:93
  340.6 1.2 multiply_subtract_fusion.2
  342.4 5.4 gather_fusion.5
  347.9 2.2 convert_element_type.325
  350.6 1.6 copy-done.3
  352.2 2.3 multiply_add_fusion.10
  357.6 4.1 gather_fusion
  361.7 2.7 convert_select_fusion.2
  364.4 5.3 gather_fusion.1
  369.8 5.4 gather_fusion.2
  375.2 4.1 gather_fusion.3
  379.3 5.4 gather_fusion.4
  384.7 6.7 %multiply_add_fusion.9 = (f32[8,256,512]{2,1,0:T(8,128)}, f32[8,256,512]{2,1,0:T(8,128)S(1)}) fusion(bf16[8,256,512]{2,1,0:T(8,128)(2,1)} %gather_fusion.1, bf16[8,256,512]{2,1,0:T(8,128)(2,1)} %gather_fusion.2, f32[256]{0:T(256)S(1)} %get-tuple-element.514, pred[8]{0:T(512)(128)(4,1)S(1)} %add_compare_fusion.2, pred[8]{0:T(512)(128)(4,1)S(1)} %fusion.88, ...), kind=kLoop, calls=%fused_computation.11.clone.1 | loop fusion | flops 11534336 | bytes 16778264 | tf_op jit(solution)/shard_map/while/body/eval_jaxpr/add | solution.py:93
  391.4 1.2 multiply_subtract_fusion.2
  393.3 5.4 gather_fusion.5
  398.7 2.2 convert_element_type.325
  401.5 1.6 copy-done.3
  403.1 2.3 multiply_add_fusion.10
  408.5 4.1 gather_fusion
  412.6 2.7 convert_select_fusion.2
  415.3 5.3 gather_fusion.1
  420.6 5.4 gather_fusion.2
  426.1 4.1 gather_fusion.3
  430.2 5.4 gather_fusion.4
  435.6 6.7 %multiply_add_fusion.9 = (f32[8,256,512]{2,1,0:T(8,128)}, f32[8,256,512]{2,1,0:T(8,128)S(1)}) fusion(bf16[8,256,512]{2,1,0:T(8,128)(2,1)} %gather_fusion.1, bf16[8,256,512]{2,1,0:T(8,128)(2,1)} %gather_fusion.2, f32[256]{0:T(256)S(1)} %get-tuple-element.514, pred[8]{0:T(512)(128)(4,1)S(1)} %add_compare_fusion.2, pred[8]{0:T(512)(128)(4,1)S(1)} %fusion.88, ...), kind=kLoop, calls=%fused_computation.11.clone.1 | loop fusion | flops 11534336 | bytes 16778264 | tf_op jit(solution)/shard_map/while/body/eval_jaxpr/add | solution.py:93
  442.3 1.2 multiply_subtract_fusion.2
  444.1 5.4 gather_fusion.5
  449.6 2.2 convert_element_type.325
  452.4 1.6 copy-done.3
  454.0 2.3 multiply_add_fusion.10
  459.3 4.1 gather_fusion
  463.4 2.7 convert_select_fusion.2
  466.1 5.3 gather_fusion.1
  471.5 5.4 gather_fusion.2
  476.9 4.1 gather_fusion.3
  481.0 5.4 gather_fusion.4
  486.4 6.7 %multiply_add_fusion.9 = (f32[8,256,512]{2,1,0:T(8,128)}, f32[8,256,512]{2,1,0:T(8,128)S(1)}) fusion(bf16[8,256,512]{2,1,0:T(8,128)(2,1)} %gather_fusion.1, bf16[8,256,512]{2,1,0:T(8,128)(2,1)} %gather_fusion.2, f32[256]{0:T(256)S(1)} %get-tuple-element.514, pred[8]{0:T(512)(128)(4,1)S(1)} %add_compare_fusion.2, pred[8]{0:T(512)(128)(4,1)S(1)} %fusion.88, ...), kind=kLoop, calls=%fused_computation.11.clone.1 | loop fusion | flops 11534336 | bytes 16778264 | tf_op jit(solution)/shard_map/while/body/eval_jaxpr/add | solution.py:93
  493.1 1.2 multiply_subtract_fusion.2
  495.0 5.4 gather_fusion.5
  500.4 2.2 convert_element_type.325
  503.2 1.6 copy-done.3
  504.8 2.3 multiply_add_fusion.10
  510.2 1.9 multiply_convert_fusion
  512.1 4.0 convolution_convert_fusion
  516.2 1.1 fusion.46
  517.3 1.1 fusion.22
  518.5 38.4 %reduce-scatter.2.cloned.1.call-done = bf16[128,512]{1,0:T(8,128)(2,1)} async-done(((bf16[128,4096]{1,0:T(8,128)(2,1)}), bf16[128,512]{1,0:T(8,128)(2,1)}) %reduce-scatter.2.cloned.1.call-update) | async-done | bytes 131088 | tf_op jit(solution)/shard_map/reduce_scatter | solution.py:149
  (182 shorter events, 21.7 us)
Async XLA Ops:
  7.2 53.0 %copy-start = (bf16[128,512]{1,0:T(8,128)(2,1)S(1)}, bf16[128,512]{1,0:T(8,128)(2,1)}, u32[]{:S(2)}) copy-start(bf16[128,512]{1,0:T(8,128)(2,1)} %param.11) | copy-start | bytes 393220
  7.2 47.2 %all-gather.9.cloned.1.call-start = ((), (), s32[]{:S(2)}) async-start(), calls=%async_computation.2 | async-start | bytes 1179648 | tf_op jit(solution)/shard_map/all_gather | solution.py:127
  7.9 133.3 %all-gather.11.cloned.1.call-start = ((), (), s32[]{:S(2)}) async-start(), calls=%async_computation.4 | async-start | bytes 8650752 | tf_op jit(solution)/shard_map/all_gather | solution.py:137
  11.5 46.9 %copy-start.15 = (bf16[128,512]{1,0:T(8,128)(2,1)S(1)}, bf16[128,512]{1,0:T(8,128)(2,1)}, u32[]{:S(2)}) copy-start(bf16[128,512]{1,0:T(8,128)(2,1)} %param.8) | copy-start | bytes 393220
  11.5 216.0 %all-gather.13.cloned.1.call-start = ((), (), s32[]{:S(2)}) async-start(), calls=%async_computation.5 | async-start | bytes 8650752 | tf_op jit(solution)/shard_map/all_gather | solution.py:139
  58.4 0.7 copy-start.10
  60.1 246.6 %all-gather.7.cloned.1.call-start = ((), (), s32[]{:S(2)}) async-start(), calls=%async_computation.1 | async-start | bytes 8650752 | tf_op jit(solution)/shard_map/all_gather | solution.py:138
  61.3 495.6 %reduce-scatter.2.cloned.1.call-start = ((), (), s32[]{:S(2)}) async-start(), calls=%async_computation.3 | async-start | bytes 1179648 | tf_op jit(solution)/shard_map/reduce_scatter | solution.py:149
  306.7 203.5 %copy-start.11 = (f32[128,512]{1,0:T(8,128)S(1)}, f32[128,512]{1,0:T(8,128)}, u32[]{:S(2)}) copy-start(f32[128,512]{1,0:T(8,128)} %copy-done.10) | copy-start | bytes 786436
  306.7 203.5 %copy-start.12 = (f32[256,128]{1,0:T(8,128)S(1)}, f32[256,128]{1,0:T(8,128)}, u32[]{:S(2)}) copy-start(f32[256,128]{1,0:T(8,128)} %get-tuple-element.404) | copy-start | bytes 393220
  333.8 6.7 %copy-start.2 = (f32[8,256,512]{2,1,0:T(8,128)S(1)}, f32[8,256,512]{2,1,0:T(8,128)}, u32[]{:S(2)}) copy-start(f32[8,256,512]{2,1,0:T(8,128)} %convert_select_fusion.2) | copy-start | bytes 12582916 | tf_op jit(solution)/shard_map/while
  350.1 2.2 copy-start.3
  355.1 1.0 copy-start.4
  355.1 1.2 copy-start.7
  356.6 0.8 copy-start.5
  356.6 1.0 copy-start.8
  384.7 6.7 %copy-start.2 = (f32[8,256,512]{2,1,0:T(8,128)S(1)}, f32[8,256,512]{2,1,0:T(8,128)}, u32[]{:S(2)}) copy-start(f32[8,256,512]{2,1,0:T(8,128)} %convert_select_fusion.2) | copy-start | bytes 12582916 | tf_op jit(solution)/shard_map/while
  400.9 2.2 copy-start.3
  405.9 1.0 copy-start.4
  405.9 1.2 copy-start.7
  407.5 0.8 copy-start.5
  407.5 1.0 copy-start.8
  435.6 6.7 %copy-start.2 = (f32[8,256,512]{2,1,0:T(8,128)S(1)}, f32[8,256,512]{2,1,0:T(8,128)}, u32[]{:S(2)}) copy-start(f32[8,256,512]{2,1,0:T(8,128)} %convert_select_fusion.2) | copy-start | bytes 12582916 | tf_op jit(solution)/shard_map/while
  451.8 2.2 copy-start.3
  456.8 1.0 copy-start.4
  456.8 1.2 copy-start.7
  458.3 0.8 copy-start.5
  458.3 1.0 copy-start.8
  486.4 6.7 %copy-start.2 = (f32[8,256,512]{2,1,0:T(8,128)S(1)}, f32[8,256,512]{2,1,0:T(8,128)}, u32[]{:S(2)}) copy-start(f32[8,256,512]{2,1,0:T(8,128)} %convert_select_fusion.2) | copy-start | bytes 12582916 | tf_op jit(solution)/shard_map/while
  502.6 2.2 copy-start.3
  507.6 1.0 copy-start.4
  507.6 1.2 copy-start.7
  509.2 0.8 copy-start.5
  509.2 1.0 copy-start.8
  512.1 4.1 copy-start.9
  512.1 4.1 copy-start.13
  512.1 4.1 copy-start.14
  512.1 44.8 %copy-start.1 = (bf16[128,512]{1,0:T(8,128)(2,1)S(1)}, bf16[128,512]{1,0:T(8,128)(2,1)}, u32[]{:S(2)}) copy-start(bf16[128,512]{1,0:T(8,128)(2,1)} %param.11) | copy-start | bytes 393220
  516.1 1.2 copy-start.6
  516.1 1.2 copy-start.16
  516.1 1.2 copy-start.17
Sparse Core Ops, SparseCore 0:
  9.8 44.5 all-gather.8
  56.9 84.3 all-gather.10
  143.7 83.7 all-gather.12
  229.9 76.7 all-gather.6
  516.3 40.5 reduce-scatter.1
where the time goes:
time: 565 us; the launch traced here: 563 us
  waiting for transfers between devices  302 us (53%)
  local copies, waits for them, and re-layouts  156 us (28%)
  other arithmetic  72.6 us (13%)
  matrix products  17.8 us (3%)
  between operations  14 us (2%)
    gather x16, local copies, waits for them, and re-layouts, fetch(): picked = spec[jnp.clip(indices, 0, block_count - 1)].astype(jnp.float32)  80.8 us
    all_gather x1, waiting for transfers between devices, per_device(): lax.all_gather(own_u, 'seq', axis=0, tiled=True)  78.3 us
    all_gather x1, waiting for transfers between devices, per_device(): lax.all_gather(own_g, 'seq', axis=0, tiled=True)  74.7 us
    all_gather x1, waiting for transfers between devices, per_device(): lax.all_gather(own_h, 'seq', axis=0, tiled=True)  67.1 us
    all_gather x1, waiting for transfers between devices, per_device(): lax.all_gather(out_grad, 'ch', axis=1, tiled=True)  42.8 us
    reduce_scatter x1, waiting for transfers between devices, per_device(): lax.psum_scatter(partial_out.astype(jnp.bfloat16), 'ch', scatter_dimensio...  38.4 us
    add x4, other arithmetic, group_step(): ahead = g_lead + shift_sign * g_next  26.7 us
    unnamed x26, local copies, waits for them, and re-layouts  24.2 us
  transfers between devices with their start and end apart: 5, of which 5 were waited for; matrix products, arithmetic and copies ran while one was open for 7% of the time, Pallas kernels for 0%

commit v1 on v0

--- a/solution.py
+++ b/solution.py
@@ -124,7 +124,9 @@
     table_high, table_low = split_table(forward_t)
     product = (key_act.astype(jnp.float32) * value_act.astype(jnp.float32)).astype(jnp.bfloat16)
     gated_grad = lax.dot_general(
-        lax.all_gather(out_grad, "ch", axis=1, tiled=True),
+        jnp.concatenate(
+            lax.all_to_all(jnp.stack([out_grad] * lax.psum(1, "ch"), 0), "ch", 0, 0), 1
+        ),
         out_weight,
         (((1,), (1,)), ((), ())),
         preferred_element_type=jnp.float32,

time: 565 us -> 526 us (0.931)
  waiting for transfers between devices: 302 us -> 239 us
  blocking collectives: 0 us -> 23.8 us
    all_gather x1 -> x0, waiting for transfers between devices: 42.8 us -> none  [per_device(): lax.all_gather(out_grad, 'ch', axis=1, tiled=True)]
    all_to_all x0 -> x1, blocking collectives: none -> 23.8 us  [per_device(): lax.all_to_all(jnp.stack([out_grad] * lax.psum(1, 'ch'), 0), 'ch', 0, 0)]
    all_gather x1, waiting for transfers between devices: 78.3 us -> 58.1 us  [per_device(): lax.all_gather(own_u, 'seq', axis=0, tiled=True)]
    unnamed x26 -> x29, local copies, waits for them, and re-layouts: 24.2 us -> 24 us
  transfers between devices with their start and end apart: 5 -> 4, of which waited for: 5 -> 4; matrix products, arithmetic and copies ran while one was open for 7% -> 6% of each run, Pallas kernels for 0% -> 0%
where the time goes in v1:
time: 526 us; the launch traced here: 524 us
  waiting for transfers between devices  239 us (45%)
  local copies, waits for them, and re-layouts  156 us (30%)
  other arithmetic  72.6 us (14%)
  blocking collectives  23.8 us (5%)
  matrix products  17.5 us (3%)
  between operations  14 us (3%)
    gather x16, local copies, waits for them, and re-layouts, fetch(): picked = spec[jnp.clip(indices, 0, block_count - 1)].astype(jnp.float32)  80.8 us
    all_gather x1, waiting for transfers between devices, per_device(): lax.all_gather(own_g, 'seq', axis=0, tiled=True)  74.9 us
    all_gather x1, waiting for transfers between devices, per_device(): lax.all_gather(own_h, 'seq', axis=0, tiled=True)  67.3 us
    all_gather x1, waiting for transfers between devices, per_device(): lax.all_gather(own_u, 'seq', axis=0, tiled=True)  58.1 us
    reduce_scatter x1, waiting for transfers between devices, per_device(): lax.psum_scatter(partial_out.astype(jnp.bfloat16), 'ch', scatter_dimensio...  38.3 us
    add x4, other arithmetic, group_step(): ahead = g_lead + shift_sign * g_next  26.8 us
    unnamed x29, local copies, waits for them, and re-layouts  24 us
    all_to_all x1, blocking collectives, per_device(): lax.all_to_all(jnp.stack([out_grad] * lax.psum(1, 'ch'), 0), 'ch', 0, 0)  23.8 us
  transfers between devices with their start and end apart: 4, of which 4 were waited for; matrix products, arithmetic and copies ran while one was open for 6% of the time, Pallas kernels for 0%

profile of v1, /device:TPU:2, one launch (start us, length us, event | category | flops | bytes accessed | tf_op | source)
XLA Modules:
  0.0 523.6 jit_solution(6561821379767867094)
XLA Ops:
  7.6 1.2 fusion.43
  8.8 1.9 fusion.19
  11.1 23.8 %all_to_all.5 = bf16[8,128,512]{1,2,0:T(8,128)(2,1)S(1)} all-to-all(bf16[8,128,512]{1,2,0:T(8,128)(2,1)S(1)} %stack.2), channel_id=1, replica_groups=mesh['seq'=32,'ch'=8] {'ch'}, dimensions={0} | all-to-all | bytes 2097152 | tf_op jit(solution)/shard_map/all_to_all | solution.py:128
  34.9 3.7 fusion.62
  41.9 1.2 multiply_select_fusion
  43.1 58.1 %all-gather.8.cloned.1.call-done = bf16[1,8192,512]{1,2,0:T(8,128)(2,1)} async-done(((bf16[1,256,512]{1,2,0:T(8,128)(2,1)}), bf16[1,8192,512]{1,2,0:T(8,128)(2,1)}) %all-gather.8.cloned.1.call-update) | async-done | bytes 8388624 | tf_op jit(solution)/shard_map/all_gather | solution.py:139
  101.2 11.4 %copy.16 = bf16[1,8192,512]{2,1,0:T(8,128)(2,1)} copy(bf16[1,8192,512]{1,2,0:T(8,128)(2,1)} %all-gather.8.cloned.1.call-done) | data formatting | bytes 16777216
  112.5 74.9 %all-gather.10.cloned.1.call-done = bf16[1,8192,512]{1,2,0:T(8,128)(2,1)} async-done(((bf16[1,256,512]{1,2,0:T(8,128)(2,1)}), bf16[1,8192,512]{1,2,0:T(8,128)(2,1)}) %all-gather.10.cloned.1.call-update) | async-done | bytes 8388624 | tf_op jit(solution)/shard_map/all_gather | solution.py:141
  187.5 12.0 %copy.17 = bf16[1,8192,512]{2,1,0:T(8,128)(2,1)} copy(bf16[1,8192,512]{1,2,0:T(8,128)(2,1)} %all-gather.10.cloned.1.call-done) | data formatting | bytes 16777216
  199.5 67.3 %all-gather.6.cloned.1.call-done = bf16[8192,512]{1,0:T(8,128)(2,1)} async-done(((bf16[256,512]{1,0:T(8,128)(2,1)}), bf16[8192,512]{1,0:T(8,128)(2,1)}) %all-gather.6.cloned.1.call-update) | async-done | bytes 8388624 | tf_op jit(solution)/shard_map/all_gather | solution.py:140
  266.8 203.6 %while.21 = (s32[]{:T(128)}, f32[256,512]{1,0:T(8,128)S(1)}, f32[256,512]{1,0:T(8,128)}, f32[256,512]{1,0:T(8,128)}, bf16[32,256,512]{2,1,0:T(8,128)(2,1)}, /*in...) while((s32[]{:T(128)}, f32[256,512]{1,0:T(8,128)S(1)}, ...), condition=%wide.region_4.5_spmd.clone.clone, body=%wide.region_0.4_spmd.clone.clone.sunk | while | flops 38148044 | bytes 155214800 | solution.py:98
  266.8 4.1 gather_fusion
  270.9 2.7 convert_select_fusion.2
  273.6 5.3 %gather_fusion.1 = bf16[8,256,512]{2,1,0:T(8,128)(2,1)} fusion(bf16[32,256,512]{2,1,0:T(8,128)(2,1)} %get-tuple-element.526, s32[1024]{0:T(1024)S(1)} %pad_clamp_fusion.11), kind=kCustom, calls=%fused_computation.5.clone.clone.1 | custom fusion | bytes 4194336 | tf_op jit(solution)/shard_map/while/body/eval_jaxpr/gather | solution.py:76
  279.0 5.4 %gather_fusion.2 = bf16[8,256,512]{2,1,0:T(8,128)(2,1)} fusion(bf16[32,256,512]{2,1,0:T(8,128)(2,1)} %get-tuple-element.526, s32[1024]{0:T(1024)S(1)} %pad_clamp_fusion.12), kind=kCustom, calls=%fused_computation.4.clone.clone.1 | custom fusion | bytes 4194336 | tf_op jit(solution)/shard_map/while/body/eval_jaxpr/gather | solution.py:76
  284.5 4.1 gather_fusion.3
  288.6 5.4 %gather_fusion.4 = bf16[8,256,512]{2,1,0:T(8,128)(2,1)} fusion(bf16[32,256,512]{2,1,0:T(8,128)(2,1)} %get-tuple-element.522, s32[1024]{0:T(1024)S(1)} %pad_clamp_fusion.14), kind=kCustom, calls=%fused_computation.clone.clone.1 | custom fusion | bytes 4194336 | tf_op jit(solution)/shard_map/while/body/eval_jaxpr/gather | solution.py:76
  293.9 6.7 %multiply_add_fusion.9 = (f32[8,256,512]{2,1,0:T(8,128)}, f32[8,256,512]{2,1,0:T(8,128)S(1)}) fusion(bf16[8,256,512]{2,1,0:T(8,128)(2,1)} %gather_fusion.1, bf16[8,256,512]{2,1,0:T(8,128)(2,1)} %gather_fusion.2, f32[256]{0:T(256)S(1)} %get-tuple-element.523, pred[8]{0:T(512)(128)(4,1)S(1)} %add_compare_fusion.2, pred[8]{0:T(512)(128)(4,1)S(1)} %fusion.88, ...), kind=kLoop, calls=%fused_computation.11.clone.1 | loop fusion | flops 11534336 | bytes 16778264 | tf_op jit(solution)/shard_map/while/body/eval_jaxpr/add | solution.py:93
  300.7 1.2 multiply_subtract_fusion.2
  302.5 5.5 %gather_fusion.5 = bf16[8,256,512]{2,1,0:T(8,128)(2,1)} fusion(bf16[32,256,512]{2,1,0:T(8,128)(2,1)} %get-tuple-element.525, s32[1024]{0:T(1024)S(1)} %pad_clamp_fusion.13), kind=kCustom, calls=%fused_computation.3.clone.clone.1 | custom fusion | bytes 4194336 | tf_op jit(solution)/shard_map/while/body/eval_jaxpr/gather | solution.py:83
  308.0 2.2 convert_element_type.325
  310.8 1.6 copy-done.3
  312.4 2.3 multiply_add_fusion.10
  317.7 4.1 gather_fusion
  321.8 2.7 convert_select_fusion.2
  324.5 5.3 %gather_fusion.1 = bf16[8,256,512]{2,1,0:T(8,128)(2,1)} fusion(bf16[32,256,512]{2,1,0:T(8,128)(2,1)} %get-tuple-element.526, s32[1024]{0:T(1024)S(1)} %pad_clamp_fusion.11), kind=kCustom, calls=%fused_computation.5.clone.clone.1 | custom fusion | bytes 4194336 | tf_op jit(solution)/shard_map/while/body/eval_jaxpr/gather | solution.py:76
  329.9 5.4 %gather_fusion.2 = bf16[8,256,512]{2,1,0:T(8,128)(2,1)} fusion(bf16[32,256,512]{2,1,0:T(8,128)(2,1)} %get-tuple-element.526, s32[1024]{0:T(1024)S(1)} %pad_clamp_fusion.12), kind=kCustom, calls=%fused_computation.4.clone.clone.1 | custom fusion | bytes 4194336 | tf_op jit(solution)/shard_map/while/body/eval_jaxpr/gather | solution.py:76
  335.4 4.1 gather_fusion.3
  339.5 5.4 %gather_fusion.4 = bf16[8,256,512]{2,1,0:T(8,128)(2,1)} fusion(bf16[32,256,512]{2,1,0:T(8,128)(2,1)} %get-tuple-element.522, s32[1024]{0:T(1024)S(1)} %pad_clamp_fusion.14), kind=kCustom, calls=%fused_computation.clone.clone.1 | custom fusion | bytes 4194336 | tf_op jit(solution)/shard_map/while/body/eval_jaxpr/gather | solution.py:76
  344.8 6.7 %multiply_add_fusion.9 = (f32[8,256,512]{2,1,0:T(8,128)}, f32[8,256,512]{2,1,0:T(8,128)S(1)}) fusion(bf16[8,256,512]{2,1,0:T(8,128)(2,1)} %gather_fusion.1, bf16[8,256,512]{2,1,0:T(8,128)(2,1)} %gather_fusion.2, f32[256]{0:T(256)S(1)} %get-tuple-element.523, pred[8]{0:T(512)(128)(4,1)S(1)} %add_compare_fusion.2, pred[8]{0:T(512)(128)(4,1)S(1)} %fusion.88, ...), kind=kLoop, calls=%fused_computation.11.clone.1 | loop fusion | flops 11534336 | bytes 16778264 | tf_op jit(solution)/shard_map/while/body/eval_jaxpr/add | solution.py:93
  351.6 1.2 multiply_subtract_fusion.2
  353.4 5.5 %gather_fusion.5 = bf16[8,256,512]{2,1,0:T(8,128)(2,1)} fusion(bf16[32,256,512]{2,1,0:T(8,128)(2,1)} %get-tuple-element.525, s32[1024]{0:T(1024)S(1)} %pad_clamp_fusion.13), kind=kCustom, calls=%fused_computation.3.clone.clone.1 | custom fusion | bytes 4194336 | tf_op jit(solution)/shard_map/while/body/eval_jaxpr/gather | solution.py:83
  358.9 2.2 convert_element_type.325
  361.7 1.6 copy-done.3
  363.3 2.3 multiply_add_fusion.10
  368.6 4.1 gather_fusion
  372.7 2.7 convert_select_fusion.2
  375.4 5.3 %gather_fusion.1 = bf16[8,256,512]{2,1,0:T(8,128)(2,1)} fusion(bf16[32,256,512]{2,1,0:T(8,128)(2,1)} %get-tuple-element.526, s32[1024]{0:T(1024)S(1)} %pad_clamp_fusion.11), kind=kCustom, calls=%fused_computation.5.clone.clone.1 | custom fusion | bytes 4194336 | tf_op jit(solution)/shard_map/while/body/eval_jaxpr/gather | solution.py:76
  380.8 5.4 %gather_fusion.2 = bf16[8,256,512]{2,1,0:T(8,128)(2,1)} fusion(bf16[32,256,512]{2,1,0:T(8,128)(2,1)} %get-tuple-element.526, s32[1024]{0:T(1024)S(1)} %pad_clamp_fusion.12), kind=kCustom, calls=%fused_computation.4.clone.clone.1 | custom fusion | bytes 4194336 | tf_op jit(solution)/shard_map/while/body/eval_jaxpr/gather | solution.py:76
  386.3 4.1 gather_fusion.3
  390.4 5.4 %gather_fusion.4 = bf16[8,256,512]{2,1,0:T(8,128)(2,1)} fusion(bf16[32,256,512]{2,1,0:T(8,128)(2,1)} %get-tuple-element.522, s32[1024]{0:T(1024)S(1)} %pad_clamp_fusion.14), kind=kCustom, calls=%fused_computation.clone.clone.1 | custom fusion | bytes 4194336 | tf_op jit(solution)/shard_map/while/body/eval_jaxpr/gather | solution.py:76
  395.7 6.7 %multiply_add_fusion.9 = (f32[8,256,512]{2,1,0:T(8,128)}, f32[8,256,512]{2,1,0:T(8,128)S(1)}) fusion(bf16[8,256,512]{2,1,0:T(8,128)(2,1)} %gather_fusion.1, bf16[8,256,512]{2,1,0:T(8,128)(2,1)} %gather_fusion.2, f32[256]{0:T(256)S(1)} %get-tuple-element.523, pred[8]{0:T(512)(128)(4,1)S(1)} %add_compare_fusion.2, pred[8]{0:T(512)(128)(4,1)S(1)} %fusion.88, ...), kind=kLoop, calls=%fused_computation.11.clone.1 | loop fusion | flops 11534336 | bytes 16778264 | tf_op jit(solution)/shard_map/while/body/eval_jaxpr/add | solution.py:93
  402.4 1.2 multiply_subtract_fusion.2
  404.3 5.5 %gather_fusion.5 = bf16[8,256,512]{2,1,0:T(8,128)(2,1)} fusion(bf16[32,256,512]{2,1,0:T(8,128)(2,1)} %get-tuple-element.525, s32[1024]{0:T(1024)S(1)} %pad_clamp_fusion.13), kind=kCustom, calls=%fused_computation.3.clone.clone.1 | custom fusion | bytes 4194336 | tf_op jit(solution)/shard_map/while/body/eval_jaxpr/gather | solution.py:83
  409.8 2.2 convert_element_type.325
  412.5 1.6 copy-done.3
  414.1 2.3 multiply_add_fusion.10
  419.5 4.1 gather_fusion
  423.6 2.7 convert_select_fusion.2
  426.3 5.3 %gather_fusion.1 = bf16[8,256,512]{2,1,0:T(8,128)(2,1)} fusion(bf16[32,256,512]{2,1,0:T(8,128)(2,1)} %get-tuple-element.526, s32[1024]{0:T(1024)S(1)} %pad_clamp_fusion.11), kind=kCustom, calls=%fused_computation.5.clone.clone.1 | custom fusion | bytes 4194336 | tf_op jit(solution)/shard_map/while/body/eval_jaxpr/gather | solution.py:76
  431.7 5.4 %gather_fusion.2 = bf16[8,256,512]{2,1,0:T(8,128)(2,1)} fusion(bf16[32,256,512]{2,1,0:T(8,128)(2,1)} %get-tuple-element.526, s32[1024]{0:T(1024)S(1)} %pad_clamp_fusion.12), kind=kCustom, calls=%fused_computation.4.clone.clone.1 | custom fusion | bytes 4194336 | tf_op jit(solution)/shard_map/while/body/eval_jaxpr/gather | solution.py:76
  437.1 4.1 gather_fusion.3
  441.2 5.4 %gather_fusion.4 = bf16[8,256,512]{2,1,0:T(8,128)(2,1)} fusion(bf16[32,256,512]{2,1,0:T(8,128)(2,1)} %get-tuple-element.522, s32[1024]{0:T(1024)S(1)} %pad_clamp_fusion.14), kind=kCustom, calls=%fused_computation.clone.clone.1 | custom fusion | bytes 4194336 | tf_op jit(solution)/shard_map/while/body/eval_jaxpr/gather | solution.py:76
  446.6 6.7 %multiply_add_fusion.9 = (f32[8,256,512]{2,1,0:T(8,128)}, f32[8,256,512]{2,1,0:T(8,128)S(1)}) fusion(bf16[8,256,512]{2,1,0:T(8,128)(2,1)} %gather_fusion.1, bf16[8,256,512]{2,1,0:T(8,128)(2,1)} %gather_fusion.2, f32[256]{0:T(256)S(1)} %get-tuple-element.523, pred[8]{0:T(512)(128)(4,1)S(1)} %add_compare_fusion.2, pred[8]{0:T(512)(128)(4,1)S(1)} %fusion.88, ...), kind=kLoop, calls=%fused_computation.11.clone.1 | loop fusion | flops 11534336 | bytes 16778264 | tf_op jit(solution)/shard_map/while/body/eval_jaxpr/add | solution.py:93
  453.3 1.2 multiply_subtract_fusion.2
  455.2 5.5 %gather_fusion.5 = bf16[8,256,512]{2,1,0:T(8,128)(2,1)} fusion(bf16[32,256,512]{2,1,0:T(8,128)(2,1)} %get-tuple-element.525, s32[1024]{0:T(1024)S(1)} %pad_clamp_fusion.13), kind=kCustom, calls=%fused_computation.3.clone.clone.1 | custom fusion | bytes 4194336 | tf_op jit(solution)/shard_map/while/body/eval_jaxpr/gather | solution.py:83
  460.7 2.2 convert_element_type.325
  463.4 1.6 copy-done.3
  465.0 2.3 multiply_add_fusion.10
  470.4 1.9 multiply_convert_fusion
  472.3 4.1 convolution_convert_fusion
  476.5 1.1 fusion.46
  477.6 1.1 fusion.22
  478.7 38.3 %reduce-scatter.2.cloned.1.call-done = bf16[128,512]{1,0:T(8,128)(2,1)} async-done(((bf16[128,4096]{1,0:T(8,128)(2,1)}), bf16[128,512]{1,0:T(8,128)(2,1)}) %reduce-scatter.2.cloned.1.call-update) | async-done | bytes 131088 | tf_op jit(solution)/shard_map/reduce_scatter | solution.py:151
  (184 shorter events, 21.3 us)
Async XLA Ops:
  7.2 33.2 %copy-start = (bf16[128,512]{1,0:T(8,128)(2,1)S(1)}, bf16[128,512]{1,0:T(8,128)(2,1)}, u32[]{:S(2)}) copy-start(bf16[128,512]{1,0:T(8,128)(2,1)} %param.11) | copy-start | bytes 393220
  7.2 3.6 copy-start.18
  7.2 94.0 %all-gather.8.cloned.1.call-start = ((), (), s32[]{:S(2)}) async-start(), calls=%async_computation.4 | async-start | bytes 8650752 | tf_op jit(solution)/shard_map/all_gather | solution.py:139
  10.8 176.7 %all-gather.10.cloned.1.call-start = ((), (), s32[]{:S(2)}) async-start(), calls=%async_computation.5 | async-start | bytes 8650752 | tf_op jit(solution)/shard_map/all_gather | solution.py:141
  34.9 3.8 copy-start.15
  38.6 0.7 copy-start.10
  40.3 226.4 %all-gather.6.cloned.1.call-start = ((), (), s32[]{:S(2)}) async-start(), calls=%async_computation.2 | async-start | bytes 8650752 | tf_op jit(solution)/shard_map/all_gather | solution.py:140
  41.6 475.5 %reduce-scatter.2.cloned.1.call-start = ((), (), s32[]{:S(2)}) async-start(), calls=%async_computation.3 | async-start | bytes 1179648 | tf_op jit(solution)/shard_map/reduce_scatter | solution.py:151
  266.8 203.6 %copy-start.11 = (f32[128,512]{1,0:T(8,128)S(1)}, f32[128,512]{1,0:T(8,128)}, u32[]{:S(2)}) copy-start(f32[128,512]{1,0:T(8,128)} %copy-done.10) | copy-start | bytes 786436
  266.8 203.6 %copy-start.12 = (f32[256,128]{1,0:T(8,128)S(1)}, f32[256,128]{1,0:T(8,128)}, u32[]{:S(2)}) copy-start(f32[256,128]{1,0:T(8,128)} %get-tuple-element.413) | copy-start | bytes 393220
  293.9 6.7 %copy-start.2 = (f32[8,256,512]{2,1,0:T(8,128)S(1)}, f32[8,256,512]{2,1,0:T(8,128)}, u32[]{:S(2)}) copy-start(f32[8,256,512]{2,1,0:T(8,128)} %convert_select_fusion.2) | copy-start | bytes 12582916 | tf_op jit(solution)/shard_map/while
  310.2 2.2 copy-start.3
  315.2 1.0 copy-start.4
  315.2 1.2 copy-start.7
  316.7 0.8 copy-start.5
  316.8 1.0 copy-start.8
  344.8 6.7 %copy-start.2 = (f32[8,256,512]{2,1,0:T(8,128)S(1)}, f32[8,256,512]{2,1,0:T(8,128)}, u32[]{:S(2)}) copy-start(f32[8,256,512]{2,1,0:T(8,128)} %convert_select_fusion.2) | copy-start | bytes 12582916 | tf_op jit(solution)/shard_map/while
  361.1 2.2 copy-start.3
  366.1 1.0 copy-start.4
  366.1 1.2 copy-start.7
  367.6 0.8 copy-start.5
  367.6 1.0 copy-start.8
  395.7 6.7 %copy-start.2 = (f32[8,256,512]{2,1,0:T(8,128)S(1)}, f32[8,256,512]{2,1,0:T(8,128)}, u32[]{:S(2)}) copy-start(f32[8,256,512]{2,1,0:T(8,128)} %convert_select_fusion.2) | copy-start | bytes 12582916 | tf_op jit(solution)/shard_map/while
  411.9 2.2 copy-start.3
  417.0 1.0 copy-start.4
  417.0 1.2 copy-start.7
  418.5 0.8 copy-start.5
  418.5 1.0 copy-start.8
  446.6 6.7 %copy-start.2 = (f32[8,256,512]{2,1,0:T(8,128)S(1)}, f32[8,256,512]{2,1,0:T(8,128)}, u32[]{:S(2)}) copy-start(f32[8,256,512]{2,1,0:T(8,128)} %convert_select_fusion.2) | copy-start | bytes 12582916 | tf_op jit(solution)/shard_map/while
  462.8 2.2 copy-start.3
  467.8 1.0 copy-start.4
  467.9 1.2 copy-start.7
  469.4 0.8 copy-start.5
  469.4 1.0 copy-start.8
  472.3 4.1 copy-start.9
  472.3 4.1 copy-start.13
  472.3 4.1 copy-start.14
  472.3 44.7 %copy-start.1 = (bf16[128,512]{1,0:T(8,128)(2,1)S(1)}, bf16[128,512]{1,0:T(8,128)(2,1)}, u32[]{:S(2)}) copy-start(bf16[128,512]{1,0:T(8,128)(2,1)} %param.11) | copy-start | bytes 393220
  476.4 1.2 copy-start.6
  476.4 1.2 copy-start.16
  476.4 1.2 copy-start.17
Sparse Core Ops, SparseCore 0:
  10.9 90.2 all-gather.7
  103.6 83.7 all-gather.9
  190.0 76.6 all-gather.5
  476.5 40.4 reduce-scatter.1
